TPU v7x, 32 devices: a whole 2x2x4 slice. The times are simulated.
32 devices in a mesh: grp: 2 (over y), inp: 8 (over z, x), freq: 2 (over core).
Axes of the slice: x: 2, y: 2, z: 4, core: 2. Of those that a mesh axis runs over, the one named last changes fastest.
Arguments:
- voltages: int32 [2048, 64, 2048], P(('grp', 'inp'), 'freq'), parts along dimension 0, may hold values from -127 to 127, as said below
- coeffs: int32 [8, 2048], replicated, may hold values from -6144 to 6144, as said below
Outputs:
- visibilities: bfloat16 [1024, 2, 36, 128, 128], P(('grp', 'inp', 'freq')), parts along dimension 0
There are 2 independent parts, one for each index of `grp`. A program takes and returns all parts, laid end to end along the dimension named above; an argument that names none is the same for every part. Nothing has to cross between parts.
Inputs may be any that keep to these rules, and one draw needn't show every extreme that they name: `voltages`: signed 8-bit samples. `coeffs`: integer coefficients.
All inputs are finite; a program needn't handle non-finite values.
Results may differ from a plain program's by a relative error of at most 0.0069.
Values may be sent and summed in bfloat16 or wider, within the bound.
A program may use at most 384 MiB of HBM per device.

v0:
```python
import math

import jax
import jax.numpy as jnp
from jax import lax
from jax.sharding import PartitionSpec as P

SPF = 2048
TAPS = 8
CH = 512
CH0 = 256
INPUTS = 1024
BLK = 128


def passed_along(x, axis, by):
    length = lax.axis_size(axis)
    pairs = [(i, i + by) for i in range(length) if 0 <= i + by < length]
    return lax.ppermute(x, axis, pairs)


def make_table():
    sample = jnp.arange(SPF, dtype=jnp.int32)[:, None]
    channel = jnp.arange(CH, dtype=jnp.int32)[None, :] + CH0
    phase = sample * channel % SPF
    angle = phase.astype(jnp.float32) * (2.0 * math.pi / SPF)
    return jnp.concatenate([jnp.cos(angle), -jnp.sin(angle)], axis=1).astype(jnp.bfloat16)


def per_device(voltages, coeffs):
    inputs_here = voltages.shape[0]
    frames_here = voltages.shape[1]
    inp_count = lax.axis_size("inp")
    freq_count = lax.axis_size("freq")
    frames_all = frames_here * freq_count
    history = voltages[:, frames_here - (TAPS - 1) :, :].astype(jnp.bfloat16)
    earlier = passed_along(history, "freq", 1)
    extended = jnp.concatenate([earlier.astype(jnp.float32), voltages.astype(jnp.float32)], axis=1)
    weights = coeffs.astype(jnp.float32)
    summed = jnp.zeros((inputs_here, frames_here, SPF), jnp.float32)
    for tap_index in range(TAPS):
        begin = TAPS - 1 - tap_index
        summed = summed + weights[tap_index] * extended[:, begin : begin + frames_here, :]
    filtered = summed.astype(jnp.bfloat16).reshape(inputs_here * frames_here, SPF)
    spectrum_t = jnp.einsum("nj,rn->jr", make_table(), filtered, preferred_element_type=jnp.float32)
    spectrum_t = spectrum_t.reshape(2 * CH, inputs_here, frames_here)
    squares = jnp.sum(spectrum_t * spectrum_t, axis=(0, 2))
    power = lax.psum(squares, "freq") / (frames_all * CH)
    gains = 1.0 / jnp.sqrt(power + 1e-06)
    scaled = (spectrum_t * gains[None, :, None]).astype(jnp.bfloat16)
    scaled = scaled.reshape(2, CH, inputs_here * frames_here)
    arrived = lax.all_to_all(scaled[None], ("inp", "freq"), split_axis=2, concat_axis=0, tiled=True)
    width_here = arrived.shape[-2]
    arranged = arrived.reshape(inp_count, freq_count, 2, width_here, inputs_here, frames_here)
    arranged = jnp.transpose(arranged, (3, 0, 4, 2, 1, 5))
    stacked = arranged.reshape(width_here, INPUTS, 2 * frames_all)
    other = jnp.concatenate([-stacked[:, :, frames_all:], stacked[:, :, :frames_all]], axis=2)
    block_count = INPUTS // BLK
    scale = 1.0 / frames_all
    pieces = []
    for row_index in range(block_count):
        row_panel = stacked[:, row_index * BLK : (row_index + 1) * BLK]
        real_part = jnp.einsum(
            "cut,cmt->cum",
            row_panel,
            stacked[:, row_index * BLK :],
            preferred_element_type=jnp.float32,
        )
        imag_part = jnp.einsum(
            "cut,cmt->cum",
            row_panel,
            other[:, row_index * BLK :],
            preferred_element_type=jnp.float32,
        )
        band = jnp.stack([real_part, imag_part], axis=1) * scale
        for col_index in range(row_index, block_count):
            begin = (col_index - row_index) * BLK
            pieces.append(band[:, :, :, begin : begin + BLK])
    return jnp.stack(pieces, axis=2).astype(jnp.bfloat16)


def solution(mesh):
    in_specs = (P(("grp", "inp"), "freq", None), P())
    out_specs = P(("grp", "inp", "freq"), None, None, None, None)
    return jax.shard_map(
        per_device, mesh=mesh, in_specs=in_specs, out_specs=out_specs, check_vma=False
    )
```

profile of v0, /device:TPU:1, one launch (start us, length us, event | category | flops | bytes accessed | tf_op | source)
XLA Modules:
  0.0 860.9 jit_solution(8330098738441136342)
XLA Ops:
  0.0 4.4 slice.335
  4.4 3.9 copy_convert_fusion
  9.9 23.3 %convert_element_type.25 = f32[128,32,2048]{2,1,0:T(8,128)} convert(s32[128,32,2048]{2,1,0:T(8,128)} %param.2) | non-fusion elementwise | flops 8388608 | bytes 67108864 | tf_op jit(solution)/shard_map/convert_element_type | solution.py:38
  33.3 18.8 %cosine_convert_fusion = (bf16[2048,512]{0,1:T(8,128)(2,1)S(1)}, bf16[2048,512]{0,1:T(8,128)(2,1)}) fusion(s32[512]{0:T(512)S(1)} %iota_add_fusion), kind=kLoop, calls=%fused_computation.94 | loop fusion | flops 17825792 | bytes 4196352 | tf_op jit(solution)/shard_map/convert.107
  52.1 5.5 copy.77
  57.6 108.5 %fusion.4 = bf16[128,32,2048]{2,1,0:T(8,128)(2,1)} fusion(f32[128,32,2048]{2,1,0:T(8,128)} %convert_element_type.25, f32[128,7,2048]{2,1,0:T(8,128)} %copy.77, f32[2048]{0:T(1024)S(1)} %bitcast.225, f32[2048]{0:T(1024)S(1)} %bitcast.226, f32[2048]{0:T(1024)S(1)} %bitcast.227, f32[2048]{0:T(1024)S(1)} %bitcast.228, f32[2048]{0:T(1024)S(1)} %bitcast.229, ...), kind=kLoop, calls=%fused_computation.16 | loop fusion | flops 192937984 | bytes 57737216 | tf_op jit(solution)/shard_map/convert_element_type | solution.py:44
  166.1 32.8 %multiply_reduce_fusion = (f32[128]{0:T(128)S(1)}, f32[1024,128,32]{1,0,2:T(8,128)}) fusion(bf16[128,32,2048]{2,1,0:T(8,128)(2,1)} %fusion.4, bf16[2048,512]{0,1:T(8,128)(2,1)} %get-tuple-element.16, bf16[2048,512]{0,1:T(8,128)(2,1)S(1)} %get-tuple-element.15), kind=kOutput, calls=%fused_computation.47 | convolution fusion | flops 17196646400 | bytes 37749248 | tf_op jit(solution)/shard_map/nj,rn->jr/dot_general | solution.py:45
  198.9 3.5 psum.7
  202.4 9.2 %multiply_convert_fusion = bf16[1024,128,32]{1,0,2:T(8,128)(2,1)} fusion(f32[1024,128,32]{1,0,2:T(8,128)} %get-tuple-element.18, f32[128]{0:T(128)S(1)} %add_rsqrt_fusion), kind=kLoop, calls=%fused_computation.46 | loop fusion | flops 8388608 | bytes 25166336 | tf_op jit(solution)/shard_map/convert_element_type | solution.py:50
  211.5 12.2 %copy.79 = bf16[1024,128,32]{0,2,1:T(8,128)(2,1)} copy(bf16[1024,128,32]{1,0,2:T(8,128)(2,1)} %multiply_convert_fusion) | data formatting | bytes 16777216 | tf_op jit(solution)/shard_map/convert_element_type | solution.py:50
  223.8 14.6 %broadcast_in_dim_reshape.3 = bf16[1,2,512,4096]{2,1,3,0:T(2,128)(2,1)} reshape(bf16[1024,128,32]{0,2,1:T(8,128)(2,1)} %copy.79) | data formatting | bytes 16777216 | tf_op jit(solution)/shard_map/broadcast_in_dim;reshape | solution.py:52
  238.3 28.3 %copy.80 = bf16[1,2,512,4096]{3,1,0,2:T(2,128)(2,1)} copy(bf16[1,2,512,4096]{2,1,3,0:T(2,128)(2,1)} %broadcast_in_dim_reshape.3) | data formatting | bytes 16777216 | tf_op jit(solution)/shard_map/broadcast_in_dim;reshape | solution.py:52
  266.6 190.0 %all_to_all.15 = bf16[1,2,512,4096]{3,1,0,2:T(2,128)(2,1)} all-to-all(bf16[1,2,512,4096]{3,1,0,2:T(2,128)(2,1)} %copy.80), channel_id=1, replica_groups=mesh['grp'=2,'inp'=8,'freq'=2] {'inp','freq'}, dimensions={2} | all-to-all | bytes 16777216 | tf_op jit(solution)/shard_map/all_to_all | solution.py:52
  456.7 12.8 %copy.81 = bf16[1,2,512,4096]{3,2,1,0:T(8,128)(2,1)} copy(bf16[1,2,512,4096]{3,1,0,2:T(2,128)(2,1)} %all_to_all.15) | data formatting | bytes 16777216 | tf_op jit(solution)/shard_map/all_to_all | solution.py:52
  469.5 7.8 copy.82
  477.3 32.6 %reshape.56 = bf16[8,2,2,32,128,32]{5,4,3,2,1,0:T(8,128)(2,1)} reshape(bf16[16,1,2,32,4096]{4,3,2,0,1:T(8,128)(2,1)} %copy.82) | data formatting | bytes 16777216 | tf_op jit(solution)/shard_map/reshape | solution.py:54
  509.8 29.2 %copy.83 = bf16[32,8,128,2,2,32]{2,1,5,4,3,0:T(8,128)(2,1)} copy(bf16[32,8,128,2,2,32]{5,2,0,3,4,1:T(8,128)(2,1)} %bitcast.206) | data formatting | bytes 16777216 | tf_op jit(solution)/shard_map/transpose | solution.py:55
  539.0 13.3 %reshape.57 = bf16[32,1024,128]{1,2,0:T(8,128)(2,1)} reshape(bf16[32,8,128,2,2,32]{2,1,5,4,3,0:T(8,128)(2,1)} %copy.83) | data formatting | bytes 16777216 | tf_op jit(solution)/shard_map/reshape | solution.py:56
  552.3 7.2 fusion.173
  561.1 8.2 convolution_bitcast_fusion.1
  569.2 8.3 copy.104
  577.6 9.1 %neg.7 = bf16[32,1024,64]{2,1,0:T(8,128)(2,1)} negate(bf16[32,1024,64]{2,1,0:T(8,128)(2,1)} %copy.104) | non-fusion elementwise | flops 2097152 | bytes 8388608 | tf_op jit(solution)/shard_map/neg | solution.py:57
  586.6 8.6 %copy.105 = bf16[32,1024,64]{2,1,0:T(8,128)(2,1)} copy(bf16[32,1024,64]{1,2,0:T(8,128)(2,1)} %get-tuple-element.6) | data formatting | bytes 8388608
  595.3 18.1 %convolution_bitcast_fusion = f32[32,1,128,1024]{3,2,0,1:T(8,128)} fusion(bf16[32,1024,64]{2,1,0:T(8,128)(2,1)} %copy.105, bf16[32,1024,64]{2,1,0:T(8,128)(2,1)} %neg.7, bf16[32,1024,128]{1,2,0:T(8,128)(2,1)} %reshape.57), kind=kOutput, calls=%fused_computation.50 | convolution fusion | flops 1090519040 | bytes 34603008 | tf_op jit(solution)/shard_map/cut,cmt->cum/dot_general | solution.py:69
  613.4 15.4 %convolution_bitcast_fusion.2 = f32[32,1,128,896]{3,2,0,1:T(8,128)} fusion(bf16[32,1024,64]{2,1,0:T(8,128)(2,1)} %copy.105, bf16[32,1024,64]{2,1,0:T(8,128)(2,1)} %neg.7, bf16[32,1024,128]{1,2,0:T(8,128)(2,1)} %reshape.57), kind=kOutput, calls=%fused_computation.52 | convolution fusion | flops 954204160 | bytes 32505856 | tf_op jit(solution)/shard_map/cut,cmt->cum/dot_general | solution.py:69
  628.8 11.2 %convolution_bitcast_fusion.3 = f32[32,1,128,896]{3,2,0,1:T(8,128)} fusion(bf16[32,1024,128]{1,2,0:T(8,128)(2,1)} %reshape.57), kind=kOutput, calls=%fused_computation.53 | convolution fusion | flops 939524096 | bytes 23068672 | tf_op jit(solution)/shard_map/cut,cmt->cum/dot_general | solution.py:63
  640.0 10.6 %fusion.50 = f32[32,1,128,768]{3,2,0,1:T(8,128)} fusion(bf16[32,1024,64]{2,1,0:T(8,128)(2,1)} %copy.105, bf16[32,1024,64]{2,1,0:T(8,128)(2,1)} %neg.7, bf16[32,1024,128]{1,2,0:T(8,128)(2,1)} %reshape.57), kind=kOutput, calls=%fused_computation.78 | convolution fusion | flops 817889280 | bytes 30408704 | tf_op jit(solution)/shard_map/cut,cmt->cum/dot_general | solution.py:69
  650.6 6.3 fusion.47
  656.9 9.9 %fusion.68 = f32[32,1,128,640]{3,2,0,1:T(8,128)} fusion(bf16[32,1024,64]{2,1,0:T(8,128)(2,1)} %copy.105, bf16[32,1024,64]{2,1,0:T(8,128)(2,1)S(1)} %bitcast.203, bf16[32,1024,128]{1,2,0:T(8,128)(2,1)S(1)} %bitcast.201), kind=kOutput, calls=%fused_computation.98 | convolution fusion | flops 681574400 | bytes 24117248 | tf_op jit(solution)/shard_map/cut,cmt->cum/dot_general | solution.py:69
  666.9 5.5 fusion.71
  672.4 8.5 fusion.77
  680.9 4.6 fusion.74
  685.4 7.1 fusion.89
  692.5 3.7 fusion.86
  696.2 3.6 convolution_bitcast_fusion.4
  699.7 2.8 convolution_bitcast_fusion.5
  702.6 2.2 convolution_bitcast_fusion.6
  704.8 2.0 convolution_bitcast_fusion.7
  706.8 13.2 %fusion.21 = bf16[32,2,128,1024]{3,2,0,1:T(8,128)(2,1)S(1)} fusion(f32[32,1,128,1024]{3,2,0,1:T(8,128)} %convolution_bitcast_fusion, f32[32,1,128,1024]{3,2,0,1:T(8,128)} %convolution_bitcast_fusion.1), kind=kLoop, calls=%fused_computation.35 | loop fusion | flops 25165824 | bytes 50331648 | tf_op jit(solution)/shard_map/convert.105
  721.9 1.9 fusion.130
  723.9 1.9 fusion.129
  725.8 1.9 fusion.128
  729.6 2.0 fusion.126
  735.4 10.3 %fusion.22 = bf16[32,2,128,896]{3,2,0,1:T(8,128)(2,1)S(1)} fusion(f32[32,1,128,896]{3,2,0,1:T(8,128)S(1)} %bitcast.208, f32[32,1,128,896]{3,2,0,1:T(8,128)} %convolution_bitcast_fusion.3), kind=kLoop, calls=%fused_computation.37 | loop fusion | flops 22020096 | bytes 44040192 | tf_op jit(solution)/shard_map/convert.89
  758.1 3.5 fusion.23
  772.0 7.0 fusion.24
  787.8 2.5 fusion.25
  811.0 49.6 %copy.101 = bf16[32,2,36,128,128]{4,3,2,1,0:T(8,128)(2,1)} copy(bf16[32,2,36,128,128]{4,3,0,1,2:T(8,128)(2,1)} %fusion.92) | data formatting | bytes 150994944 | tf_op jit(solution)/shard_map/stack | solution.py:79
  (117 shorter events, 63.0 us)
Async XLA Ops:
  8.3 25.0 %copy-start.5 = (s32[8,2048]{1,0:T(8,128)S(1)}, s32[8,2048]{1,0:T(8,128)}, u32[]{:S(2)}) copy-start(s32[8,2048]{1,0:T(8,128)} %param.3) | copy-start | bytes 196612
  8.3 43.8 %collective-permute-start = (bf16[128,7,2048]{2,0,1:T(8,128)(2,1)S(1)}, bf16[128,7,2048]{2,0,1:T(8,128)(2,1)S(1)}, u32[]{:S(2)}, u32[]{:S(2)}) collective-permute-start(bf16[128,7,2048]{2,0,1:T(8,128)(2,1)S(1)} %copy_convert_fusion), channel_id=1, source_target_pairs={{0,1},{2,3},{4,5},{6,7},{8,9},{10,11},{12,13},{14,15},{16,17},{18,... | collective-permute-start | bytes 11010056 | tf_op jit(solution)/shard_map/ppermute | solution.py:19
  552.3 8.8 %copy-start = (bf16[32,1024,128]{1,2,0:T(8,128)(2,1)S(1)}, bf16[32,1024,128]{1,2,0:T(8,128)(2,1)}, u32[]{:S(2)}) copy-start(bf16[32,1024,128]{1,2,0:T(8,128)(2,1)} %reshape.57) | copy-start | bytes 25165828
  628.7 21.8 %slice-start = ((s8[8388608]{0:T(1024)(128)(4,1)}), s8[4194304]{0:T(1024)(128)(4,1)S(1)}, s32[]{:S(2)}) async-start(s8[8388608]{0:T(1024)(128)(4,1)} %bitcast.200), calls=%async_computation.1 | async-start | bytes 8388608
  628.7 28.2 %slice-start.2 = ((s8[8388608]{0:T(1024)(128)(4,1)}), s8[4194304]{0:T(1024)(128)(4,1)S(1)}, s32[]{:S(2)}) async-start(s8[8388608]{0:T(1024)(128)(4,1)} %bitcast.202), calls=%async_computation.3 | async-start | bytes 8388608
  640.0 10.6 %slice-start.1 = ((s8[8388608]{0:T(1024)(128)(4,1)}), s8[4194304]{0:T(1024)(128)(4,1)S(1)}, s32[]{:S(2)}) async-start(s8[8388608]{0:T(1024)(128)(4,1)} %bitcast.200), calls=%async_computation.2 | async-start | bytes 8388608
  640.0 17.0 %slice-start.3 = ((s8[8388608]{0:T(1024)(128)(4,1)}), s8[4194304]{0:T(1024)(128)(4,1)S(1)}, s32[]{:S(2)}) async-start(s8[8388608]{0:T(1024)(128)(4,1)} %bitcast.202), calls=%async_computation.4 | async-start | bytes 8388608
  680.9 15.3 %slice-start.4 = ((s8[8388608]{0:T(1024)(128)(4,1)}), s8[4194304]{0:T(1024)(128)(4,1)S(1)}, s32[]{:S(2)}) async-start(s8[8388608]{0:T(1024)(128)(4,1)} %bitcast.204), calls=%async_computation.5 | async-start | bytes 8388608
  685.4 10.7 %slice-start.5 = ((s8[8388608]{0:T(1024)(128)(4,1)}), s8[4194304]{0:T(1024)(128)(4,1)S(1)}, s32[]{:S(2)}) async-start(s8[8388608]{0:T(1024)(128)(4,1)} %bitcast.204), calls=%async_computation.6 | async-start | bytes 8388608
  721.9 13.4 %slice-start.6 = ((s8[14680064]{0:T(1024)(128)(4,1)}), s8[4194304]{0:T(1024)(128)(4,1)S(1)}, s32[]{:S(2)}) async-start(s8[14680064]{0:T(1024)(128)(4,1)} %bitcast.207), calls=%async_computation.7 | async-start | bytes 8388608
  723.9 11.5 %slice-start.7 = ((s8[14680064]{0:T(1024)(128)(4,1)}), s8[4194304]{0:T(1024)(128)(4,1)S(1)}, s32[]{:S(2)}) async-start(s8[14680064]{0:T(1024)(128)(4,1)} %bitcast.207), calls=%async_computation.8 | async-start | bytes 8388608
  727.7 7.6 slice-start.8
  731.6 3.7 slice-start.9
  735.4 22.6 %slice-start.13 = ((s8[12582912]{0:T(1024)(128)(4,1)}), s8[4194304]{0:T(1024)(128)(4,1)S(1)}, s32[]{:S(2)}) async-start(s8[12582912]{0:T(1024)(128)(4,1)} %bitcast.211), calls=%async_computation.14 | async-start | bytes 8388608
  735.4 22.6 %slice-start.14 = ((s8[12582912]{0:T(1024)(128)(4,1)}), s8[4194304]{0:T(1024)(128)(4,1)S(1)}, s32[]{:S(2)}) async-start(s8[12582912]{0:T(1024)(128)(4,1)} %bitcast.211), calls=%async_computation.15 | async-start | bytes 8388608
  747.5 10.5 %slice-start.10 = ((s8[12582912]{0:T(1024)(128)(4,1)}), s8[4194304]{0:T(1024)(128)(4,1)S(1)}, s32[]{:S(2)}) async-start(s8[12582912]{0:T(1024)(128)(4,1)} %bitcast.209), calls=%async_computation.11 | async-start | bytes 8388608
  747.5 10.5 %slice-start.15 = ((s8[12582912]{0:T(1024)(128)(4,1)}), s8[4194304]{0:T(1024)(128)(4,1)S(1)}, s32[]{:S(2)}) async-start(s8[12582912]{0:T(1024)(128)(4,1)} %bitcast.211), calls=%async_computation.16 | async-start | bytes 8388608
  751.0 7.0 slice-start.11
  754.5 3.5 slice-start.12
  763.2 8.7 %slice-start.16 = ((s8[10485760]{0:T(1024)(128)(4,1)}), s8[4194304]{0:T(1024)(128)(4,1)S(1)}, s32[]{:S(2)}) async-start(s8[10485760]{0:T(1024)(128)(4,1)} %bitcast.213), calls=%async_computation.17 | async-start | bytes 8388608
  765.0 7.0 slice-start.17
  768.5 3.5 slice-start.18
  770.2 17.5 %slice-start.21 = ((s8[8388608]{0:T(1024)(128)(4,1)}), s8[4194304]{0:T(1024)(128)(4,1)S(1)}, s32[]{:S(2)}) async-start(s8[8388608]{0:T(1024)(128)(4,1)} %bitcast.217), calls=%async_computation.22 | async-start | bytes 8388608
  772.0 15.7 %slice-start.22 = ((s8[8388608]{0:T(1024)(128)(4,1)}), s8[4194304]{0:T(1024)(128)(4,1)S(1)}, s32[]{:S(2)}) async-start(s8[8388608]{0:T(1024)(128)(4,1)} %bitcast.217), calls=%async_computation.23 | async-start | bytes 8388608
  780.8 6.9 slice-start.19
  784.2 3.5 slice-start.20
  785.9 11.4 %slice-start.25 = ((s8[6291456]{0:T(1024)(128)(4,1)}), s8[4194304]{0:T(1024)(128)(4,1)S(1)}, s32[]{:S(2)}) async-start(s8[6291456]{0:T(1024)(128)(4,1)} %bitcast.222), calls=%async_computation.26 | async-start | bytes 8388608
  787.7 9.6 %slice-start.26 = ((s8[6291456]{0:T(1024)(128)(4,1)}), s8[2097152]{0:T(1024)(128)(4,1)S(1)}, s32[]{:S(2)}) async-start(s8[6291456]{0:T(1024)(128)(4,1)} %bitcast.222), calls=%async_computation.27 | async-start | bytes 4194304
  790.3 7.0 slice-start.23
  793.8 3.5 slice-start.24
  799.2 5.2 copy-start.1
  799.2 5.2 copy-start.2
  804.5 4.7 copy-start.3
  804.5 4.7 copy-start.4
where the time goes:
time: 869 us; the launch traced here: 861 us
  local copies, waits for them, and re-layouts  299 us (34%)
  other arithmetic  214 us (25%)
  blocking collectives  193 us (22%)
  matrix products  152 us (17%)
    all_to_all x1, blocking collectives, per_device(): lax.all_to_all(scaled[None], ('inp', 'freq'), split_axis=2, concat_axis=0...  190 us
    convert_element_type x1, other arithmetic, per_device(): summed.astype(jnp.bfloat16).reshape(inputs_here * frames_here, SPF)  109 us
    unnamed x103, local copies, waits for them, and re-layouts  81.1 us
    dot_general x8, matrix products, per_device(): jnp.einsum('cut,cmt->cum', row_panel, other[:, row_index * BLK:], preferr...  75.3 us
    another operation x9, other arithmetic  62.2 us
    another operation x1, local copies, waits for them, and re-layouts, per_device(): return jnp.stack(pieces, axis=2).astype(jnp.bfloat16)  49.6 us
    dot_general x8, matrix products, per_device(): jnp.einsum('cut,cmt->cum', row_panel, stacked[:, row_index * BLK:], prefe...  44.3 us
    another operation x2, local copies, waits for them, and re-layouts, per_device(): scaled[None]  42.9 us
  transfers between devices with their start and end apart: 1, of which 0 were waited for; matrix products, arithmetic and copies ran while one was open for 5% of the time, Pallas kernels for 0%

commit v1 on v0

--- a/solution.py
+++ b/solution.py
@@ -1,8 +1,12 @@
+import functools
 import math
 
 import jax
 import jax.numpy as jnp
+import numpy as np
 from jax import lax
+from jax.experimental import pallas as pl
+from jax.experimental.pallas import tpu as pltpu
 from jax.sharding import PartitionSpec as P
 
 SPF = 2048
@@ -27,7 +31,7 @@
     return jnp.concatenate([jnp.cos(angle), -jnp.sin(angle)], axis=1).astype(jnp.bfloat16)
 
 
-def per_device(voltages, coeffs):
+def plain_device(voltages, coeffs):
     inputs_here = voltages.shape[0]
     frames_here = voltages.shape[1]
     inp_count = lax.axis_size("inp")
@@ -79,6 +83,382 @@
     return jnp.stack(pieces, axis=2).astype(jnp.bfloat16)
 
 
+MESH = pl.DeviceIdType.MESH
+GROUP = 8
+LANE = 128
+HALF = 16
+PLANE = 4
+
+
+def table_rows(count):
+    sample = np.arange(SPF, dtype=np.int32)[None, :]
+    channel = np.arange(CH, dtype=np.int32)[:, None] + CH0
+    angle = (sample * channel % SPF).astype(np.float32) * np.float32(2.0 * math.pi / SPF)
+    both = np.stack([np.cos(angle), -np.sin(angle)])
+    rows = both.reshape(2, count, CH // count, SPF).transpose(1, 0, 2, 3).reshape(2 * CH, SPF)
+    return jnp.asarray(rows.astype(jnp.bfloat16))
+
+
+def front_kernel(
+    inp_count,
+    freq_count,
+    volts,
+    coeffs,
+    table_hbm,
+    spec,
+    arrived,
+    powers,
+    frames,
+    history,
+    table,
+    filtered,
+    spread,
+    staged,
+    power,
+    load_sem,
+    table_sem,
+    hist_send,
+    hist_recv,
+    stage_sem,
+    send_sem,
+    recv_sem,
+    pow_sem,
+    pow_send,
+    pow_recv,
+):
+    grp = lax.axis_index("grp")
+    inp = lax.axis_index("inp")
+    freq = lax.axis_index("freq")
+    count = inp_count * freq_count
+    me = inp * freq_count + freq
+    inputs_here, frames_here, _ = volts.shape
+    halves = frames_here // HALF
+    taps = coeffs.shape[0]
+    per_owner = spec.shape[2]
+    rows = PLANE * per_owner
+    planes = count // PLANE
+
+    def where(index):
+        return (grp, index // freq_count, index % freq_count)
+
+    def load(t):
+        return pltpu.make_async_copy(volts.at[:, t, :], frames.at[t], load_sem.at[t])
+
+    half_order = list(reversed(range(halves)))
+    fetch_order = []
+    for half in half_order:
+        for t in range(max(0, half * HALF - taps + 1), (half + 1) * HALF):
+            if t not in fetch_order:
+                fetch_order.append(t)
+    for t in fetch_order:
+        load(t).start()
+    table_copy = pltpu.make_async_copy(table_hbm, table, table_sem)
+    table_copy.start()
+
+    barrier = pltpu.get_barrier_semaphore()
+
+    def greet(step, carry):
+        other = (me + step) % count
+        pl.semaphore_signal(barrier, inc=1, device_id=where(other), device_id_type=MESH)
+        return carry
+
+    lax.fori_loop(1, count, greet, 0)
+    power[...] = jnp.zeros_like(power)
+    pl.semaphore_wait(barrier, count - 1)
+
+    def history_copy(step):
+        return pltpu.make_async_remote_copy(
+            src_ref=volts.at[:, frames_here - taps + 1 + step, :],
+            dst_ref=history.at[step],
+            send_sem=hist_send.at[step],
+            recv_sem=hist_recv.at[step],
+            device_id=(grp, inp, 1),
+            device_id_type=MESH,
+        )
+
+    @pl.when(freq == 0)
+    def _():
+        for step in range(taps - 1):
+            history_copy(step).start()
+        history[...] = jnp.zeros_like(history)
+
+    loaded = set()
+
+    def filter_group(first, base):
+        def tile(index, carry):
+            lanes = SPF // LANE
+            row = pl.multiple_of(index // lanes * 16, 16)
+            col = pl.multiple_of(index % lanes * LANE, LANE)
+
+            def sample(t):
+                if t < 0:
+                    return history[taps - 1 + t, pl.ds(row, 16), pl.ds(col, LANE)].astype(jnp.float32)
+                return frames[t, pl.ds(row, 16), pl.ds(col, LANE)].astype(jnp.float32)
+
+            window = {t: sample(t) for t in range(first - taps + 1, first + GROUP)}
+            weights = [coeffs[k, :, pl.ds(col, LANE)] for k in range(taps)]
+            for t in range(first, first + GROUP):
+                total = weights[0] * window[t]
+                for k in range(1, taps):
+                    total = total + weights[k] * window[t - k]
+                at = pl.multiple_of((t - base) * inputs_here + row, 16)
+                filtered[pl.ds(at, 16), pl.ds(col, LANE)] = total.astype(jnp.bfloat16)
+            return carry
+
+        lax.fori_loop(0, inputs_here // 16 * (SPF // LANE), tile, 0)
+
+    def remote(half, other):
+        return pltpu.make_async_remote_copy(
+            src_ref=spec.at[other, half],
+            dst_ref=arrived.at[me, half],
+            send_sem=send_sem.at[half, other],
+            recv_sem=recv_sem.at[half, me],
+            device_id=where(other),
+            device_id_type=MESH,
+        )
+
+    plane_here = me // PLANE
+    if planes == 4:
+        order = [
+            (plane_here + 2) % 4,
+            3 - plane_here,
+            plane_here + 1 - 2 * (plane_here % 2),
+            plane_here,
+        ]
+    else:
+        order = [(plane_here + planes // 2 + step) % planes for step in range(planes)]
+
+    frames_step = 4
+    for half_number, half in enumerate(half_order):
+        for first in range(half * HALF, (half + 1) * HALF, GROUP):
+            for t in range(max(0, first - taps + 1), first + GROUP):
+                if t not in loaded:
+                    loaded.add(t)
+                    load(t).wait()
+            if first == 0:
+
+                @pl.when(freq != 0)
+                def _():
+                    for step in range(taps - 1):
+                        history_copy(step).wait_recv()
+
+            filter_group(first, half * HALF)
+        if half_number == 0:
+            table_copy.wait()
+        for plane in order:
+
+            def transform(step, carry):
+                lines = table[pl.ds(pl.multiple_of(plane * rows, rows), rows), :]
+                at = pl.multiple_of(step * (frames_step * inputs_here), frames_step * inputs_here)
+                chunk = filtered[pl.ds(at, frames_step * inputs_here), :]
+                product = lax.dot_general(
+                    lines, chunk, (((1,), (1,)), ((), ())), preferred_element_type=jnp.float32
+                )
+                total = jnp.zeros((8, LANE), jnp.float32)
+                for t in range(frames_step):
+                    piece = product[:, t * LANE : (t + 1) * LANE]
+                    spread[pl.ds(step * frames_step + t, rows, stride=HALF), :] = piece
+                    total = total + jnp.sum((piece * piece).reshape(rows // 8, 8, LANE), axis=0)
+                power[...] += total
+                return carry
+
+            lax.fori_loop(0, HALF // frames_step, transform, 0)
+
+            def convert(step, carry):
+                at = pl.multiple_of(step * (per_owner * HALF), per_owner * HALF)
+                block = spread[pl.ds(at, per_owner * HALF), :].astype(jnp.bfloat16)
+                staged[step] = block.reshape(per_owner, HALF, LANE)
+                return carry
+
+            lax.fori_loop(0, PLANE, convert, 0)
+
+            def put_away(step, start):
+                owner = plane * PLANE + step
+                away = pltpu.make_async_copy(staged.at[step], spec.at[owner, half], stage_sem.at[step])
+                here = pltpu.make_async_copy(staged.at[step], arrived.at[owner, half], stage_sem.at[step])
+
+                @pl.when(owner != me)
+                def _():
+                    if start:
+                        away.start()
+                    else:
+                        away.wait()
+                        remote(half, owner).start()
+
+                @pl.when(owner == me)
+                def _():
+                    if start:
+                        here.start()
+                    else:
+                        here.wait()
+
+            for step in range(PLANE):
+                put_away(step, True)
+            for step in range(PLANE):
+                put_away(step, False)
+
+    power_copy = pltpu.make_async_copy(power, powers.at[me], pow_sem)
+    power_copy.start()
+    power_copy.wait()
+
+    def power_remote(other):
+        return pltpu.make_async_remote_copy(
+            src_ref=powers.at[me],
+            dst_ref=powers.at[me],
+            send_sem=pow_send.at[other],
+            recv_sem=pow_recv.at[me],
+            device_id=where(other),
+            device_id_type=MESH,
+        )
+
+    def send_power(step, carry):
+        power_remote((me + step) % count).start()
+        return carry
+
+    lax.fori_loop(1, count, send_power, 0)
+
+    @pl.when(freq == 0)
+    def _():
+        for step in range(taps - 1):
+            history_copy(step).wait_send()
+
+    def finish(step, carry):
+        other = (me + step) % count
+        for half in range(halves):
+            remote(half, other).wait_send()
+            pltpu.make_async_remote_copy(
+                src_ref=spec.at[other, half],
+                dst_ref=arrived.at[other, half],
+                send_sem=send_sem.at[half, other],
+                recv_sem=recv_sem.at[half, other],
+                device_id=where(other),
+                device_id_type=MESH,
+            ).wait_recv()
+        power_remote(other).wait_send()
+        pltpu.make_async_remote_copy(
+            src_ref=powers.at[other],
+            dst_ref=powers.at[other],
+            send_sem=pow_send.at[other],
+            recv_sem=pow_recv.at[other],
+            device_id=where(other),
+            device_id_type=MESH,
+        ).wait_recv()
+        return carry
+
+    lax.fori_loop(1, count, finish, 0)
+
+
+def front(voltages, coeffs, inp_count, freq_count):
+    inputs_here, frames_here, _ = voltages.shape
+    taps = coeffs.shape[0]
+    count = inp_count * freq_count
+    per_owner = 2 * CH // count
+    halves = frames_here // HALF
+    wide = jnp.broadcast_to(coeffs.astype(jnp.float32)[:, None, :], (taps, 16, SPF))
+    anywhere = pl.BlockSpec(memory_space=pl.ANY)
+    blocks = jax.ShapeDtypeStruct((count, halves, per_owner, HALF, LANE), jnp.bfloat16)
+    _, arrived, powers = pl.pallas_call(
+        functools.partial(front_kernel, inp_count, freq_count),
+        out_shape=(blocks, blocks, jax.ShapeDtypeStruct((count, 8, LANE), jnp.float32)),
+        in_specs=[anywhere, pl.BlockSpec(memory_space=pltpu.VMEM), anywhere],
+        out_specs=(anywhere, anywhere, anywhere),
+        scratch_shapes=[
+            pltpu.VMEM((frames_here, inputs_here, SPF), jnp.int32),
+            pltpu.VMEM((taps - 1, inputs_here, SPF), jnp.int32),
+            pltpu.VMEM((2 * CH, SPF), jnp.bfloat16),
+            pltpu.VMEM((HALF * inputs_here, SPF), jnp.bfloat16),
+            pltpu.VMEM((PLANE * per_owner * HALF, LANE), jnp.float32),
+            pltpu.VMEM((PLANE, per_owner, HALF, LANE), jnp.bfloat16),
+            pltpu.VMEM((8, LANE), jnp.float32),
+            pltpu.SemaphoreType.DMA((frames_here,)),
+            pltpu.SemaphoreType.DMA,
+            pltpu.SemaphoreType.DMA((taps - 1,)),
+            pltpu.SemaphoreType.DMA((taps - 1,)),
+            pltpu.SemaphoreType.DMA((PLANE,)),
+            pltpu.SemaphoreType.DMA((halves, count)),
+            pltpu.SemaphoreType.DMA((halves, count)),
+            pltpu.SemaphoreType.DMA,
+            pltpu.SemaphoreType.DMA((count,)),
+            pltpu.SemaphoreType.DMA((count,)),
+        ],
+        compiler_params=pltpu.CompilerParams(
+            collective_id=0, has_side_effects=True, vmem_limit_bytes=67043328
+        ),
+        name="front",
+    )(voltages, wide, table_rows(count))
+    return arrived, powers
+
+
+def correlate_kernel(block, gain_row, gain_col, out, turned):
+    panels, freq_count, halves = block.shape[:3]
+    order = [(f, h) for f in range(freq_count) for h in range(halves)]
+    straight, crossed = [], []
+    for panel in range(panels):
+        real = jnp.concatenate([block[panel, f, h, 0, 0] for f, h in order], axis=0)
+        imag = jnp.concatenate([block[panel, f, h, 1, 0] for f, h in order], axis=0)
+        both = jnp.concatenate([real, imag], axis=0)
+        straight.append(both)
+        crossed.append(jnp.concatenate([-imag, real], axis=0))
+        turned[panel * BLK : (panel + 1) * BLK, :] = both.T
+    for col in range(panels):
+        weights = jnp.concatenate([straight[col], crossed[col]], axis=1)
+        product = jnp.dot(
+            turned[: (col + 1) * BLK, :], weights, preferred_element_type=jnp.float32
+        )
+        for row in range(col + 1):
+            pair = row * panels - row * (row - 1) // 2 + col - row
+            gain = gain_col[row * BLK : (row + 1) * BLK, :] * gain_row[col : col + 1, :]
+            part = product[row * BLK : (row + 1) * BLK]
+            out[0, 0, pair] = (part[:, :BLK] * gain).astype(jnp.bfloat16)
+            out[0, 1, pair] = (part[:, BLK:] * gain).astype(jnp.bfloat16)
+
+
+def correlate(arrived, gains, inp_count, freq_count, frames_all):
+    count, halves, per_owner, _, _ = arrived.shape
+    width = per_owner // 2
+    pairs = inp_count * (inp_count + 1) // 2
+    blocks = arrived.reshape(inp_count, freq_count, halves, 2, width, HALF, LANE)
+    column = jnp.broadcast_to((gains * (1.0 / frames_all)).reshape(-1, 1), (inp_count * BLK, BLK))
+    return pl.pallas_call(
+        correlate_kernel,
+        grid=(width,),
+        out_shape=jax.ShapeDtypeStruct((width, 2, pairs, BLK, BLK), jnp.bfloat16),
+        in_specs=[
+            pl.BlockSpec(
+                (inp_count, freq_count, halves, 2, 1, HALF, LANE), lambda c: (0, 0, 0, 0, c, 0, 0)
+            ),
+            pl.BlockSpec((inp_count, BLK), lambda c: (0, 0)),
+            pl.BlockSpec((inp_count * BLK, BLK), lambda c: (0, 0)),
+        ],
+        out_specs=pl.BlockSpec((1, 2, pairs, BLK, BLK), lambda c: (c, 0, 0, 0, 0)),
+        scratch_shapes=[pltpu.VMEM((inp_count * BLK, 2 * frames_all), jnp.bfloat16)],
+        compiler_params=pltpu.CompilerParams(vmem_limit_bytes=48 * 1024 * 1024),
+        name="correlate",
+    )(blocks, gains, column)
+
+
+def per_device(voltages, coeffs):
+    inputs_here, frames_here, _ = voltages.shape
+    inp_count = lax.axis_size("inp")
+    freq_count = lax.axis_size("freq")
+    count = inp_count * freq_count
+    frames_all = frames_here * freq_count
+    fits = (
+        inputs_here == BLK
+        and freq_count == 2
+        and frames_here % HALF == 0
+        and count % PLANE == 0
+        and CH % count == 0
+        and 2 * frames_all % LANE == 0
+    )
+    if not fits:
+        return plain_device(voltages, coeffs)
+    arrived, powers = front(voltages, coeffs, inp_count, freq_count)
+    power = jnp.sum(powers.reshape(inp_count, freq_count * 8, LANE), axis=1) / (frames_all * CH)
+    gains = 1.0 / jnp.sqrt(power + 1e-06)
+    return correlate(arrived, gains, inp_count, freq_count, frames_all)
+
+
 def solution(mesh):
     in_specs = (P(("grp", "inp"), "freq", None), P())
     out_specs = P(("grp", "inp", "freq"), None, None, None, None)

time: 869 us -> 264 us (0.30)
  local copies, waits for them, and re-layouts: 299 us -> 1.26 us
  Pallas kernels: 0 us -> 260 us
  other arithmetic: 214 us -> 1.73 us
  blocking collectives: 193 us -> 0 us
  matrix products: 152 us -> 0 us
    pallas_call x0 -> x2, Pallas kernels: none -> 260 us  [the longest x1 222 us: front(): pl.pallas_call(functools.partial(front_kernel, inp_count, freq_count), ou...]
    all_to_all x1 -> x0, blocking collectives: 190 us -> none  [per_device(): lax.all_to_all(scaled[None], ('inp', 'freq'), split_axis=2, concat_axis=0...]
    dot_general x17 -> x0, matrix products: 152 us -> none  [the longest x8 75.3 us: per_device(): jnp.einsum('cut,cmt->cum', row_panel, other[:, row_index * BLK:], preferr...]
    convert_element_type x4 -> x1, other arithmetic: 141 us -> 0.84 us  [front(): coeffs.astype(jnp.float32)[:, None, :]]
    another operation x3 -> x0, local copies, waits for them, and re-layouts: 92.4 us -> none  [the longest x1 49.6 us: per_device(): return jnp.stack(pieces, axis=2).astype(jnp.bfloat16)]
    unnamed x103 -> x0, local copies, waits for them, and re-layouts: 81.1 us -> none
    another operation x10 -> x0, other arithmetic: 64.1 us -> none
    reshape x2 -> x0, local copies, waits for them, and re-layouts: 45.9 us -> none  [the longest x1 32.6 us: per_device(): arrived.reshape(inp_count, freq_count, 2, width_here, inputs_here, frames...]
  transfers between devices with their start and end apart: 1 -> 0, of which waited for: 0 -> 0; matrix products, arithmetic and copies ran while one was open for 5% -> 0% of each run, Pallas kernels for 0% -> 0%
where the time goes in v1:
time: 264 us; the launch traced here: 263 us
  Pallas kernels  260 us (98%)
    pallas_call x1, Pallas kernels, front(): pl.pallas_call(functools.partial(front_kernel, inp_count, freq_count), ou...  222 us
    pallas_call x1, Pallas kernels, correlate(): pl.pallas_call(correlate_kernel, grid=(width,), out_shape=jax.ShapeDtypeS...  38 us

profile of v1, /device:TPU:1, one launch (start us, length us, event | category | flops | bytes accessed | tf_op | source)
XLA Modules:
  0.0 262.5 jit_solution(11217516645636330087)
XLA Ops:
  0.0 0.8 convert_element_type.3
  0.8 1.1 broadcast_in_dim.4.coeffs
  1.9 221.5 %front.1 = (bf16[16,2,64,16,128]{4,3,2,1,0:T(8,128)(2,1)}, bf16[16,2,64,16,128]{4,3,2,1,0:T(8,128)(2,1)}, f32[16,8,128]{2,1,0:T(8,128)}) custom-call(s32[128,32,2048]{2,1,0:T(8,128)} %volts.1, f32[8,16,2048]{2,1,0:T(8,128)} %broadcast_in_dim.4.coeffs, bf16[1024,2048]{1,0:T(8,128)(2,1)} %constant.12.clone.table_hbm), custom_call_target="tpu_custom_call" | custom-call | tf_op jit(solution)/shard_map/front/pallas_call | solution.py:360
  223.4 0.9 reduce_sum.10
  224.3 0.2 broadcast_in_dim.5.gain_col
  224.5 38.0 %correlate.1 = bf16[32,2,36,128,128]{4,3,2,1,0:T(8,128)(2,1)} custom-call(bf16[8,2,2,2,32,16,128]{6,5,4,3,2,1,0:T(8,128)(2,1)} %bitcast.4, f32[8,128]{1,0:T(8,128)S(1)} %get-tuple-element.10.gain_row, f32[1024,128]{1,0:T(8,128)S(1)} %broadcast_in_dim.5.gain_col), custom_call_target="tpu_custom_call" | custom-call | tf_op jit(solution)/shard_map/correlate/pallas_call | solution.py:422
  (2 shorter events, 0.0 us)
